TPU v7x, 32 devices: a whole 2x2x4 slice. The times are simulated.
32 devices in a mesh: pair: 2 (over x), grow: 4 (over y, core), gcol: 4 (over z).
Axes of the slice: x: 2, y: 2, z: 4, core: 2. Of those that a mesh axis runs over, the one named last changes fastest.
Arguments:
- core_matrix: bfloat16 [12288, 12288], P('grow', 'gcol'), may hold values from -0.00048828125 to 0.00048828125
- pair_panels: bfloat16 [12, 32, 12288], P('pair', None, ('grow', 'gcol')), may hold values from -6 to 6
- amplitudes: bfloat16 [12, 32, 32], P('pair'), may hold values from -0.1875 to 0.1875
- pair_widths: int32 [12], P('pair'), may hold values from 8 to 32
- batch_plan: int32 [12], P('pair'), may hold values from 0 to 11, each once
Outputs:
- residual: float32 [12, 1024], P('pair', ('grow', 'gcol'))
Inputs may be any that keep to these rules, and one draw needn't show every extreme that they name: batch_plan names every pair exactly once.
All inputs are finite; a program needn't handle non-finite values.
Results may differ from a plain program's by a relative error of at most 0.015.
Values may be sent and summed in bfloat16 or wider, within the bound.
A program may use at most 64 MiB of HBM per device.

v0:
```python
import jax
import jax.numpy as jnp
from jax import lax
from jax.sharding import PartitionSpec as P


def local(core_matrix, pair_panels, amplitudes, pair_widths, batch_plan):
    depth = amplitudes.shape[1]
    live = (
        lax.broadcasted_iota(jnp.int32, (pair_widths.shape[0], depth), 1) < pair_widths[:, None]
    ).astype(jnp.bfloat16)
    masked = amplitudes * live[:, :, None] * live[:, None, :]
    row_index = lax.axis_index("grow")
    col_index = lax.axis_index("gcol")
    row_len = core_matrix.shape[0]
    col_len = core_matrix.shape[1]
    gathered = lax.all_gather(pair_panels, ("grow", "gcol"), axis=2, tiled=True)
    left = lax.dynamic_slice_in_dim(gathered, row_index * row_len, row_len, 2)
    right = lax.dynamic_slice_in_dim(gathered, col_index * col_len, col_len, 2)

    def slot_term(items):
        left_panel, right_panel, amps, mask = items
        projected = jnp.dot(amps, right_panel, preferred_element_type=jnp.float32).astype(
            jnp.bfloat16
        )
        coupled = lax.dot_general(
            left_panel, projected, (((0,), (0,)), ((), ())), preferred_element_type=jnp.float32
        ).astype(jnp.bfloat16)
        coupled = lax.optimization_barrier(coupled)
        weighted = (core_matrix.astype(jnp.float32) * coupled.astype(jnp.float32)).astype(
            jnp.bfloat16
        )
        back = lax.dot_general(
            weighted, right_panel, (((1,), (1,)), ((), ())), preferred_element_type=jnp.float32
        ).astype(jnp.bfloat16)
        partial_sum = jnp.dot(left_panel, back, preferred_element_type=jnp.float32)
        keep = mask.astype(jnp.float32)
        return (partial_sum * keep[:, None] * keep[None, :]).reshape(depth * depth)

    terms = lax.map(slot_term, (left, right, masked, live))
    total = lax.psum(terms, ("grow", "gcol"))
    share = terms.shape[1] // lax.axis_size(("grow", "gcol"))
    reduced = lax.dynamic_slice_in_dim(total, lax.axis_index(("grow", "gcol")) * share, share, 1)
    every_row = lax.all_gather(reduced, "pair", axis=0, tiled=True)
    return jnp.take(every_row, batch_plan, axis=0)


def solution(mesh):
    in_specs = (
        P("grow", "gcol"),
        P("pair", None, ("grow", "gcol")),
        P("pair", None, None),
        P("pair"),
        P("pair"),
    )
    out_specs = P("pair", ("grow", "gcol"))
    return jax.shard_map(local, mesh=mesh, in_specs=in_specs, out_specs=out_specs, check_vma=False)
```

profile of v0, /device:TPU:0, one launch (start us, length us, event | category | flops | bytes accessed | tf_op | source)
XLA Modules:
  0.0 285.3 jit_solution(8804718714653839679)
XLA Ops:
  6.5 0.0 all-gather.3.cloned.1.call-start
  6.5 0.7 all-gather.3.cloned.1.call-update
  7.3 0.7 compare_select_fusion
  8.0 0.7 compare_and_fusion
  8.6 0.7 fusion.27
  9.3 0.9 multiply_multiply_fusion
  10.2 55.5 %all-gather.3.cloned.1.call-done = bf16[6,32,12288]{2,1,0:T(8,128)(2,1)} async-done(((bf16[6,32,768]{2,1,0:T(8,128)(2,1)}), bf16[6,32,12288]{2,1,0:T(8,128)(2,1)}) %all-gather.3.cloned.1.call-update) | async-done | bytes 4718608 | tf_op jit(solution)/shard_map/all_gather | solution.py:17
  65.8 1.9 constant_dynamic-slice_fusion.1
  67.6 145.8 %while.10 = (s32[]{:T(128)}, f32[6,1024]{1,0:T(8,128)S(1)}, bf16[6,32,3072]{2,1,0:T(8,128)(2,1)S(1)}, bf16[3072,3072]{1,0:T(8,128)(2,1)}, bf16[6,32,32]{2,1,0:T(...) while((s32[]{:T(128)}, f32[6,1024]{1,0:T(8,128)S(1)}, ...), condition=%wide.region_1.2_spmd, body=%wide.region_0.1_spmd.sunk | while | flops 1267927040 | bytes 57442084 | solution.py:40
  67.6 9.3 %convolution_convert_fusion.3 = bf16[3072,3072]{1,0:T(8,128)(2,1)} fusion(bf16[6,32,3072]{2,1,0:T(8,128)(2,1)S(1)} %get-tuple-element.125, s32[]{:T(128)} %get-tuple-element.111, bf16[6,32,3072]{2,1,0:T(8,128)(2,1)S(1)} %get-tuple-element.122, bf16[6,32,32]{2,1,0:T(8,128)(2,1)S(1)} %get-tuple-element.124), kind=kOutput, calls=%fused_computation.3.clone.1 | convolution fusion | flops 619806720 | bytes 19277312 | tf_op jit(solution)/shard_map/while/body/eval_jaxpr/dot_general | solution.py:26
  77.0 14.8 %fusion.41 = f32[32,32]{1,0:T(8,128)S(1)} fusion(bf16[3072,3072]{1,0:T(8,128)(2,1)} %convolution_convert_fusion.3, bf16[3072,3072]{1,0:T(8,128)(2,1)} %get-tuple-element.123, bf16[6,32,3072]{2,1,0:T(8,128)(2,1)S(1)} %get-tuple-element.125, s32[]{:T(128)} %get-tuple-element.111, bf16[6,32,3072]{2,1,0:T(8,128)(2,1)S(1)} %get-tuple-element.122, ...), kind=kOutput, calls=%fused_computation.8.clone.1 | convolution fusion | flops 648120320 | bytes 38148096 | tf_op jit(solution)/shard_map/while/body/eval_jaxpr/dot_general | solution.py:36
  91.8 0.1 broadcast_in_dim.31
  91.8 0.1 dynamic_update_slice.5
  91.9 9.3 %convolution_convert_fusion.3 = bf16[3072,3072]{1,0:T(8,128)(2,1)} fusion(bf16[6,32,3072]{2,1,0:T(8,128)(2,1)S(1)} %get-tuple-element.125, s32[]{:T(128)} %get-tuple-element.111, bf16[6,32,3072]{2,1,0:T(8,128)(2,1)S(1)} %get-tuple-element.122, bf16[6,32,32]{2,1,0:T(8,128)(2,1)S(1)} %get-tuple-element.124), kind=kOutput, calls=%fused_computation.3.clone.1 | convolution fusion | flops 619806720 | bytes 19277312 | tf_op jit(solution)/shard_map/while/body/eval_jaxpr/dot_general | solution.py:26
  101.3 14.8 %fusion.41 = f32[32,32]{1,0:T(8,128)S(1)} fusion(bf16[3072,3072]{1,0:T(8,128)(2,1)} %convolution_convert_fusion.3, bf16[3072,3072]{1,0:T(8,128)(2,1)} %get-tuple-element.123, bf16[6,32,3072]{2,1,0:T(8,128)(2,1)S(1)} %get-tuple-element.125, s32[]{:T(128)} %get-tuple-element.111, bf16[6,32,3072]{2,1,0:T(8,128)(2,1)S(1)} %get-tuple-element.122, ...), kind=kOutput, calls=%fused_computation.8.clone.1 | convolution fusion | flops 648120320 | bytes 38148096 | tf_op jit(solution)/shard_map/while/body/eval_jaxpr/dot_general | solution.py:36
  116.1 0.1 broadcast_in_dim.31
  116.1 0.1 dynamic_update_slice.5
  116.2 9.3 %convolution_convert_fusion.3 = bf16[3072,3072]{1,0:T(8,128)(2,1)} fusion(bf16[6,32,3072]{2,1,0:T(8,128)(2,1)S(1)} %get-tuple-element.125, s32[]{:T(128)} %get-tuple-element.111, bf16[6,32,3072]{2,1,0:T(8,128)(2,1)S(1)} %get-tuple-element.122, bf16[6,32,32]{2,1,0:T(8,128)(2,1)S(1)} %get-tuple-element.124), kind=kOutput, calls=%fused_computation.3.clone.1 | convolution fusion | flops 619806720 | bytes 19277312 | tf_op jit(solution)/shard_map/while/body/eval_jaxpr/dot_general | solution.py:26
  125.6 14.8 %fusion.41 = f32[32,32]{1,0:T(8,128)S(1)} fusion(bf16[3072,3072]{1,0:T(8,128)(2,1)} %convolution_convert_fusion.3, bf16[3072,3072]{1,0:T(8,128)(2,1)} %get-tuple-element.123, bf16[6,32,3072]{2,1,0:T(8,128)(2,1)S(1)} %get-tuple-element.125, s32[]{:T(128)} %get-tuple-element.111, bf16[6,32,3072]{2,1,0:T(8,128)(2,1)S(1)} %get-tuple-element.122, ...), kind=kOutput, calls=%fused_computation.8.clone.1 | convolution fusion | flops 648120320 | bytes 38148096 | tf_op jit(solution)/shard_map/while/body/eval_jaxpr/dot_general | solution.py:36
  140.3 0.1 broadcast_in_dim.31
  140.4 0.1 dynamic_update_slice.5
  140.5 9.3 %convolution_convert_fusion.3 = bf16[3072,3072]{1,0:T(8,128)(2,1)} fusion(bf16[6,32,3072]{2,1,0:T(8,128)(2,1)S(1)} %get-tuple-element.125, s32[]{:T(128)} %get-tuple-element.111, bf16[6,32,3072]{2,1,0:T(8,128)(2,1)S(1)} %get-tuple-element.122, bf16[6,32,32]{2,1,0:T(8,128)(2,1)S(1)} %get-tuple-element.124), kind=kOutput, calls=%fused_computation.3.clone.1 | convolution fusion | flops 619806720 | bytes 19277312 | tf_op jit(solution)/shard_map/while/body/eval_jaxpr/dot_general | solution.py:26
  149.9 14.8 %fusion.41 = f32[32,32]{1,0:T(8,128)S(1)} fusion(bf16[3072,3072]{1,0:T(8,128)(2,1)} %convolution_convert_fusion.3, bf16[3072,3072]{1,0:T(8,128)(2,1)} %get-tuple-element.123, bf16[6,32,3072]{2,1,0:T(8,128)(2,1)S(1)} %get-tuple-element.125, s32[]{:T(128)} %get-tuple-element.111, bf16[6,32,3072]{2,1,0:T(8,128)(2,1)S(1)} %get-tuple-element.122, ...), kind=kOutput, calls=%fused_computation.8.clone.1 | convolution fusion | flops 648120320 | bytes 38148096 | tf_op jit(solution)/shard_map/while/body/eval_jaxpr/dot_general | solution.py:36
  164.6 0.1 broadcast_in_dim.31
  164.7 0.1 dynamic_update_slice.5
  164.8 9.3 %convolution_convert_fusion.3 = bf16[3072,3072]{1,0:T(8,128)(2,1)} fusion(bf16[6,32,3072]{2,1,0:T(8,128)(2,1)S(1)} %get-tuple-element.125, s32[]{:T(128)} %get-tuple-element.111, bf16[6,32,3072]{2,1,0:T(8,128)(2,1)S(1)} %get-tuple-element.122, bf16[6,32,32]{2,1,0:T(8,128)(2,1)S(1)} %get-tuple-element.124), kind=kOutput, calls=%fused_computation.3.clone.1 | convolution fusion | flops 619806720 | bytes 19277312 | tf_op jit(solution)/shard_map/while/body/eval_jaxpr/dot_general | solution.py:26
  174.2 14.8 %fusion.41 = f32[32,32]{1,0:T(8,128)S(1)} fusion(bf16[3072,3072]{1,0:T(8,128)(2,1)} %convolution_convert_fusion.3, bf16[3072,3072]{1,0:T(8,128)(2,1)} %get-tuple-element.123, bf16[6,32,3072]{2,1,0:T(8,128)(2,1)S(1)} %get-tuple-element.125, s32[]{:T(128)} %get-tuple-element.111, bf16[6,32,3072]{2,1,0:T(8,128)(2,1)S(1)} %get-tuple-element.122, ...), kind=kOutput, calls=%fused_computation.8.clone.1 | convolution fusion | flops 648120320 | bytes 38148096 | tf_op jit(solution)/shard_map/while/body/eval_jaxpr/dot_general | solution.py:36
  188.9 0.1 broadcast_in_dim.31
  189.0 0.1 dynamic_update_slice.5
  189.1 9.3 %convolution_convert_fusion.3 = bf16[3072,3072]{1,0:T(8,128)(2,1)} fusion(bf16[6,32,3072]{2,1,0:T(8,128)(2,1)S(1)} %get-tuple-element.125, s32[]{:T(128)} %get-tuple-element.111, bf16[6,32,3072]{2,1,0:T(8,128)(2,1)S(1)} %get-tuple-element.122, bf16[6,32,32]{2,1,0:T(8,128)(2,1)S(1)} %get-tuple-element.124), kind=kOutput, calls=%fused_computation.3.clone.1 | convolution fusion | flops 619806720 | bytes 19277312 | tf_op jit(solution)/shard_map/while/body/eval_jaxpr/dot_general | solution.py:26
  198.5 14.8 %fusion.41 = f32[32,32]{1,0:T(8,128)S(1)} fusion(bf16[3072,3072]{1,0:T(8,128)(2,1)} %convolution_convert_fusion.3, bf16[3072,3072]{1,0:T(8,128)(2,1)} %get-tuple-element.123, bf16[6,32,3072]{2,1,0:T(8,128)(2,1)S(1)} %get-tuple-element.125, s32[]{:T(128)} %get-tuple-element.111, bf16[6,32,3072]{2,1,0:T(8,128)(2,1)S(1)} %get-tuple-element.122, ...), kind=kOutput, calls=%fused_computation.8.clone.1 | convolution fusion | flops 648120320 | bytes 38148096 | tf_op jit(solution)/shard_map/while/body/eval_jaxpr/dot_general | solution.py:36
  213.2 0.1 broadcast_in_dim.31
  213.3 0.1 dynamic_update_slice.5
  213.4 59.4 %psum.7 = f32[6,1024]{1,0:T(8,128)S(1)} all-reduce(f32[6,1024]{1,0:T(8,128)S(1)} %get-tuple-element.42), channel_id=1, replica_groups=mesh['pair'=2,'grow'=4,'gcol'=4] {'grow','gcol'}, use_global_device_ids=true, to_apply=%region_2.3 | all-reduce | flops 6144 | bytes 49152 | tf_op jit(solution)/shard_map/psum | solution.py:41
  272.8 0.1 dynamic-slice_bitcast_fusion
  272.9 4.3 %all-gather = f32[2,6,64]{2,1,0:T(8,128)S(1)} all-gather(f32[1,6,64]{2,1,0:T(8,128)S(1)} %dynamic-slice_bitcast_fusion), channel_id=1, replica_groups=mesh['pair'=2,'grow'=4,'gcol'=4] {'pair'}, dimensions={0}, use_global_device_ids=true | all-gather | bytes 4608 | tf_op jit(solution)/shard_map/all_gather | solution.py:44
  277.2 0.6 gather_fusion
  277.8 0.7 broadcast_select_fusion
  (9 shorter events, 0.0 us)
Async XLA Ops:
  6.5 59.2 %all-gather.3.cloned.1.call-start = ((), (), s32[]{:S(2)}) async-start(), calls=%async_computation | async-start | bytes 5013504 | tf_op jit(solution)/shard_map/all_gather | solution.py:17
Sparse Core Ops, SparseCore 0:
  9.5 56.1 all-gather.2
where the time goes:
time: 286 us; the launch traced here: 285 us
  matrix products  145 us (51%)
  blocking collectives  63.7 us (22%)
  waiting for transfers between devices  56.2 us (20%)
  between operations  13.4 us (5%)
  other arithmetic  3.64 us (1%)
  local copies, waits for them, and re-layouts  3.44 us (1%)
    dot_general x6, matrix products, slot_term(): partial_sum = jnp.dot(left_panel, back, preferred_element_type=jnp.float32)  88.5 us
    psum x1, blocking collectives, local(): total = lax.psum(terms, ('grow', 'gcol'))  59.4 us
    dot_general x6, matrix products, slot_term(): lax.dot_general(left_panel, projected, (((0,), (0,)), ((), ())), preferre...  56.1 us
    all_gather x1, waiting for transfers between devices, local(): gathered = lax.all_gather(pair_panels, ('grow', 'gcol'), axis=2, tiled=True)  55.5 us
  transfers between devices with their start and end apart: 1, of which 1 were waited for; matrix products, arithmetic and copies ran while one was open for 1% of the time, Pallas kernels for 0%

commit v1 on v0

--- a/solution.py
+++ b/solution.py
@@ -38,7 +38,7 @@
         return (partial_sum * keep[:, None] * keep[None, :]).reshape(depth * depth)
 
     terms = lax.map(slot_term, (left, right, masked, live))
-    total = lax.psum(terms, ("grow", "gcol"))
+    total = jnp.sum(lax.all_gather(terms, ("grow", "gcol")), axis=0)
     share = terms.shape[1] // lax.axis_size(("grow", "gcol"))
     reduced = lax.dynamic_slice_in_dim(total, lax.axis_index(("grow", "gcol")) * share, share, 1)
     every_row = lax.all_gather(reduced, "pair", axis=0, tiled=True)

time: 286 us -> 261 us (0.913)
  blocking collectives: 63.7 us -> 39 us
    psum x1 -> x0, blocking collectives: 59.4 us -> none  [local(): total = lax.psum(terms, ('grow', 'gcol'))]
    all_gather x0 -> x1, blocking collectives: none -> 34.6 us  [local(): total = jnp.sum(lax.all_gather(terms, ('grow', 'gcol')), axis=0)]
where the time goes in v1:
time: 261 us
  matrix products  145 us (56%)
  waiting for transfers between devices  56.2 us (22%)
  blocking collectives  39 us (15%)
  between operations  13.4 us (5%)
  other arithmetic  3.69 us (1%)
  local copies, waits for them, and re-layouts  3.44 us (1%)
    dot_general x6, matrix products, slot_term(): partial_sum = jnp.dot(left_panel, back, preferred_element_type=jnp.float32)  88.5 us
    dot_general x6, matrix products, slot_term(): lax.dot_general(left_panel, projected, (((0,), (0,)), ((), ())), preferre...  56.1 us
    all_gather x1, waiting for transfers between devices, local(): gathered = lax.all_gather(pair_panels, ('grow', 'gcol'), axis=2, tiled=True)  55.5 us
    all_gather x1, blocking collectives, local(): total = jnp.sum(lax.all_gather(terms, ('grow', 'gcol')), axis=0)  34.6 us
  transfers between devices with their start and end apart: 1, of which 1 were waited for; matrix products, arithmetic and copies ran while one was open for 1% of the time, Pallas kernels for 0%

profile of v1, /device:TPU:0, one launch (start us, length us, event | category | flops | bytes accessed | tf_op | source)
XLA Modules:
  0.0 260.6 jit_solution(880381371381873054)
XLA Ops:
  6.5 0.0 all-gather.5.cloned.1.call-start
  6.5 0.7 all-gather.5.cloned.1.call-update
  7.3 0.7 compare_select_fusion
  8.0 0.7 compare_and_fusion
  8.6 0.7 fusion.27
  9.3 0.9 multiply_multiply_fusion
  10.2 55.5 %all-gather.5.cloned.1.call-done = bf16[6,32,12288]{2,1,0:T(8,128)(2,1)} async-done(((bf16[6,32,768]{2,1,0:T(8,128)(2,1)}), bf16[6,32,12288]{2,1,0:T(8,128)(2,1)}) %all-gather.5.cloned.1.call-update) | async-done | bytes 4718608 | tf_op jit(solution)/shard_map/all_gather | solution.py:17
  65.8 1.9 constant_dynamic-slice_fusion.1
  67.6 145.8 %while.10 = (s32[]{:T(128)}, f32[6,1024]{1,0:T(8,128)S(1)}, bf16[6,32,3072]{2,1,0:T(8,128)(2,1)S(1)}, bf16[3072,3072]{1,0:T(8,128)(2,1)}, bf16[6,32,32]{2,1,0:T(...) while((s32[]{:T(128)}, f32[6,1024]{1,0:T(8,128)S(1)}, ...), condition=%wide.region_1.2_spmd, body=%wide.region_0.1_spmd.sunk | while | flops 1267927040 | bytes 57442084 | solution.py:40
  67.6 9.3 %convolution_convert_fusion.3 = bf16[3072,3072]{1,0:T(8,128)(2,1)} fusion(bf16[6,32,3072]{2,1,0:T(8,128)(2,1)S(1)} %get-tuple-element.125, s32[]{:T(128)} %get-tuple-element.111, bf16[6,32,3072]{2,1,0:T(8,128)(2,1)S(1)} %get-tuple-element.122, bf16[6,32,32]{2,1,0:T(8,128)(2,1)S(1)} %get-tuple-element.124), kind=kOutput, calls=%fused_computation.3.clone.1 | convolution fusion | flops 619806720 | bytes 19277312 | tf_op jit(solution)/shard_map/while/body/eval_jaxpr/dot_general | solution.py:26
  77.0 14.8 %fusion.41 = f32[32,32]{1,0:T(8,128)S(1)} fusion(bf16[3072,3072]{1,0:T(8,128)(2,1)} %convolution_convert_fusion.3, bf16[3072,3072]{1,0:T(8,128)(2,1)} %get-tuple-element.123, bf16[6,32,3072]{2,1,0:T(8,128)(2,1)S(1)} %get-tuple-element.125, s32[]{:T(128)} %get-tuple-element.111, bf16[6,32,3072]{2,1,0:T(8,128)(2,1)S(1)} %get-tuple-element.122, ...), kind=kOutput, calls=%fused_computation.8.clone.1 | convolution fusion | flops 648120320 | bytes 38148096 | tf_op jit(solution)/shard_map/while/body/eval_jaxpr/dot_general | solution.py:36
  91.8 0.1 broadcast_in_dim.31
  91.8 0.1 dynamic_update_slice.5
  91.9 9.3 %convolution_convert_fusion.3 = bf16[3072,3072]{1,0:T(8,128)(2,1)} fusion(bf16[6,32,3072]{2,1,0:T(8,128)(2,1)S(1)} %get-tuple-element.125, s32[]{:T(128)} %get-tuple-element.111, bf16[6,32,3072]{2,1,0:T(8,128)(2,1)S(1)} %get-tuple-element.122, bf16[6,32,32]{2,1,0:T(8,128)(2,1)S(1)} %get-tuple-element.124), kind=kOutput, calls=%fused_computation.3.clone.1 | convolution fusion | flops 619806720 | bytes 19277312 | tf_op jit(solution)/shard_map/while/body/eval_jaxpr/dot_general | solution.py:26
  101.3 14.8 %fusion.41 = f32[32,32]{1,0:T(8,128)S(1)} fusion(bf16[3072,3072]{1,0:T(8,128)(2,1)} %convolution_convert_fusion.3, bf16[3072,3072]{1,0:T(8,128)(2,1)} %get-tuple-element.123, bf16[6,32,3072]{2,1,0:T(8,128)(2,1)S(1)} %get-tuple-element.125, s32[]{:T(128)} %get-tuple-element.111, bf16[6,32,3072]{2,1,0:T(8,128)(2,1)S(1)} %get-tuple-element.122, ...), kind=kOutput, calls=%fused_computation.8.clone.1 | convolution fusion | flops 648120320 | bytes 38148096 | tf_op jit(solution)/shard_map/while/body/eval_jaxpr/dot_general | solution.py:36
  116.1 0.1 broadcast_in_dim.31
  116.1 0.1 dynamic_update_slice.5
  116.2 9.3 %convolution_convert_fusion.3 = bf16[3072,3072]{1,0:T(8,128)(2,1)} fusion(bf16[6,32,3072]{2,1,0:T(8,128)(2,1)S(1)} %get-tuple-element.125, s32[]{:T(128)} %get-tuple-element.111, bf16[6,32,3072]{2,1,0:T(8,128)(2,1)S(1)} %get-tuple-element.122, bf16[6,32,32]{2,1,0:T(8,128)(2,1)S(1)} %get-tuple-element.124), kind=kOutput, calls=%fused_computation.3.clone.1 | convolution fusion | flops 619806720 | bytes 19277312 | tf_op jit(solution)/shard_map/while/body/eval_jaxpr/dot_general | solution.py:26
  125.6 14.8 %fusion.41 = f32[32,32]{1,0:T(8,128)S(1)} fusion(bf16[3072,3072]{1,0:T(8,128)(2,1)} %convolution_convert_fusion.3, bf16[3072,3072]{1,0:T(8,128)(2,1)} %get-tuple-element.123, bf16[6,32,3072]{2,1,0:T(8,128)(2,1)S(1)} %get-tuple-element.125, s32[]{:T(128)} %get-tuple-element.111, bf16[6,32,3072]{2,1,0:T(8,128)(2,1)S(1)} %get-tuple-element.122, ...), kind=kOutput, calls=%fused_computation.8.clone.1 | convolution fusion | flops 648120320 | bytes 38148096 | tf_op jit(solution)/shard_map/while/body/eval_jaxpr/dot_general | solution.py:36
  140.3 0.1 broadcast_in_dim.31
  140.4 0.1 dynamic_update_slice.5
  140.5 9.3 %convolution_convert_fusion.3 = bf16[3072,3072]{1,0:T(8,128)(2,1)} fusion(bf16[6,32,3072]{2,1,0:T(8,128)(2,1)S(1)} %get-tuple-element.125, s32[]{:T(128)} %get-tuple-element.111, bf16[6,32,3072]{2,1,0:T(8,128)(2,1)S(1)} %get-tuple-element.122, bf16[6,32,32]{2,1,0:T(8,128)(2,1)S(1)} %get-tuple-element.124), kind=kOutput, calls=%fused_computation.3.clone.1 | convolution fusion | flops 619806720 | bytes 19277312 | tf_op jit(solution)/shard_map/while/body/eval_jaxpr/dot_general | solution.py:26
  149.9 14.8 %fusion.41 = f32[32,32]{1,0:T(8,128)S(1)} fusion(bf16[3072,3072]{1,0:T(8,128)(2,1)} %convolution_convert_fusion.3, bf16[3072,3072]{1,0:T(8,128)(2,1)} %get-tuple-element.123, bf16[6,32,3072]{2,1,0:T(8,128)(2,1)S(1)} %get-tuple-element.125, s32[]{:T(128)} %get-tuple-element.111, bf16[6,32,3072]{2,1,0:T(8,128)(2,1)S(1)} %get-tuple-element.122, ...), kind=kOutput, calls=%fused_computation.8.clone.1 | convolution fusion | flops 648120320 | bytes 38148096 | tf_op jit(solution)/shard_map/while/body/eval_jaxpr/dot_general | solution.py:36
  164.6 0.1 broadcast_in_dim.31
  164.7 0.1 dynamic_update_slice.5
  164.8 9.3 %convolution_convert_fusion.3 = bf16[3072,3072]{1,0:T(8,128)(2,1)} fusion(bf16[6,32,3072]{2,1,0:T(8,128)(2,1)S(1)} %get-tuple-element.125, s32[]{:T(128)} %get-tuple-element.111, bf16[6,32,3072]{2,1,0:T(8,128)(2,1)S(1)} %get-tuple-element.122, bf16[6,32,32]{2,1,0:T(8,128)(2,1)S(1)} %get-tuple-element.124), kind=kOutput, calls=%fused_computation.3.clone.1 | convolution fusion | flops 619806720 | bytes 19277312 | tf_op jit(solution)/shard_map/while/body/eval_jaxpr/dot_general | solution.py:26
  174.2 14.8 %fusion.41 = f32[32,32]{1,0:T(8,128)S(1)} fusion(bf16[3072,3072]{1,0:T(8,128)(2,1)} %convolution_convert_fusion.3, bf16[3072,3072]{1,0:T(8,128)(2,1)} %get-tuple-element.123, bf16[6,32,3072]{2,1,0:T(8,128)(2,1)S(1)} %get-tuple-element.125, s32[]{:T(128)} %get-tuple-element.111, bf16[6,32,3072]{2,1,0:T(8,128)(2,1)S(1)} %get-tuple-element.122, ...), kind=kOutput, calls=%fused_computation.8.clone.1 | convolution fusion | flops 648120320 | bytes 38148096 | tf_op jit(solution)/shard_map/while/body/eval_jaxpr/dot_general | solution.py:36
  188.9 0.1 broadcast_in_dim.31
  189.0 0.1 dynamic_update_slice.5
  189.1 9.3 %convolution_convert_fusion.3 = bf16[3072,3072]{1,0:T(8,128)(2,1)} fusion(bf16[6,32,3072]{2,1,0:T(8,128)(2,1)S(1)} %get-tuple-element.125, s32[]{:T(128)} %get-tuple-element.111, bf16[6,32,3072]{2,1,0:T(8,128)(2,1)S(1)} %get-tuple-element.122, bf16[6,32,32]{2,1,0:T(8,128)(2,1)S(1)} %get-tuple-element.124), kind=kOutput, calls=%fused_computation.3.clone.1 | convolution fusion | flops 619806720 | bytes 19277312 | tf_op jit(solution)/shard_map/while/body/eval_jaxpr/dot_general | solution.py:26
  198.5 14.8 %fusion.41 = f32[32,32]{1,0:T(8,128)S(1)} fusion(bf16[3072,3072]{1,0:T(8,128)(2,1)} %convolution_convert_fusion.3, bf16[3072,3072]{1,0:T(8,128)(2,1)} %get-tuple-element.123, bf16[6,32,3072]{2,1,0:T(8,128)(2,1)S(1)} %get-tuple-element.125, s32[]{:T(128)} %get-tuple-element.111, bf16[6,32,3072]{2,1,0:T(8,128)(2,1)S(1)} %get-tuple-element.122, ...), kind=kOutput, calls=%fused_computation.8.clone.1 | convolution fusion | flops 648120320 | bytes 38148096 | tf_op jit(solution)/shard_map/while/body/eval_jaxpr/dot_general | solution.py:36
  213.2 0.1 broadcast_in_dim.31
  213.3 0.1 dynamic_update_slice.5
  213.4 34.6 %all-gather.1 = f32[16,6,1024]{2,1,0:T(8,128)S(1)} all-gather(f32[1,6,1024]{2,1,0:T(8,128)S(1)} %bitcast.36), channel_id=2, replica_groups=mesh['pair'=2,'grow'=4,'gcol'=4] {'grow','gcol'}, dimensions={0}, use_global_device_ids=true | all-gather | bytes 417792 | tf_op jit(solution)/shard_map/all_gather | solution.py:41
  248.1 0.1 dynamic-slice_bitcast_fusion
  248.1 4.3 %all-gather.2 = f32[2,6,64]{2,1,0:T(8,128)S(1)} all-gather(f32[1,6,64]{2,1,0:T(8,128)S(1)} %dynamic-slice_bitcast_fusion), channel_id=1, replica_groups=mesh['pair'=2,'grow'=4,'gcol'=4] {'pair'}, dimensions={0}, use_global_device_ids=true | all-gather | bytes 4608 | tf_op jit(solution)/shard_map/all_gather | solution.py:44
  252.5 0.6 gather_fusion
  253.0 0.7 broadcast_select_fusion
  (10 shorter events, 0.1 us)
Async XLA Ops:
  6.5 59.2 %all-gather.5.cloned.1.call-start = ((), (), s32[]{:S(2)}) async-start(), calls=%async_computation | async-start | bytes 5013504 | tf_op jit(solution)/shard_map/all_gather | solution.py:17
Sparse Core Ops, SparseCore 0:
  9.5 56.1 all-gather.4
